TPU v7x, 512 devices: a whole 4x8x8 slice. The times are simulated.
512 devices in a mesh: dp: 64 (over z, y_lo, x), tensor: 8 (over y_hi, core).
Axes of the slice: x: 4, y: 8 (y_hi: 4, y_lo: 2; y = y_hi * 2 + y_lo), z: 8, core: 2. Of those that a mesh axis runs over, the one named last changes fastest.
Arguments:
- tokens: bfloat16 [24576, 16384], P('dp', 'tensor'), may hold values from -6 to 6
- cotangent: bfloat16 [24576, 16384], P('dp', 'tensor'), may hold values from -16 to 16
- left_factor: bfloat16 [192, 16384], P('tensor'), may hold values from -0.125 to 0.125
- right_factor: bfloat16 [192, 16384], P('tensor'), may hold values from -0.125 to 0.125
- panel_rank: int32 [8], replicated, may hold values from 1 to 24, as said below
Outputs:
- token_grad: bfloat16 [24576, 16384], P('dp', 'tensor')
- left_grad: float32 [192, 8, 64, 32], P('tensor', None, 'dp')
- right_grad: float32 [192, 8, 64, 32], P('tensor', None, 'dp')
Inputs may be any that keep to these rules, and one draw needn't show every extreme that they name: panel_rank[p] counts the live slots at the start of panel p; at least one panel has all 24 slots live and another has a single live slot.
All inputs are finite; a program needn't handle non-finite values.
Results may differ from a plain program's by a relative error of at most 0.0049.
Values may be sent and summed in bfloat16 or wider, within the bound.
A program may use at most 128 MiB of HBM per device.

v0:
```python
import math

import jax
import jax.numpy as jnp
from jax import lax
from jax.sharding import PartitionSpec as P


def block_view(home):
    groups = lax.axis_size("tensor")
    width = lax.axis_size("dp")
    block = home.shape[1] // (groups * width)
    return home.reshape(home.shape[0], groups, width, block)


def own_blocks(summed):
    return lax.dynamic_slice_in_dim(summed, lax.axis_index("dp"), 1, 2)


def settle_both(left_cols, right_cols):
    left_home, right_home = (
        lax.all_to_all(left_cols, "tensor", split_axis=0, concat_axis=1, tiled=True),
        lax.all_to_all(right_cols, "tensor", split_axis=0, concat_axis=1, tiled=True),
    )
    left_home = block_view(left_home)
    right_home = block_view(right_home)
    left_sum, right_sum = lax.psum((left_home, right_home), "dp")
    return (own_blocks(left_sum), own_blocks(right_sum))


def local(tokens, cotangent, left_factor, right_factor, panel_rank):
    slot_count = left_factor.shape[0]
    groups = lax.axis_size("tensor")
    all_slots = slot_count * groups
    left_cols, right_cols = (
        lax.all_to_all(left_factor, "tensor", split_axis=1, concat_axis=0, tiled=True),
        lax.all_to_all(right_factor, "tensor", split_axis=1, concat_axis=0, tiled=True),
    )
    slots = jnp.arange(all_slots, dtype=jnp.int32)
    limits = jnp.repeat(panel_rank, slot_count, total_repeat_length=all_slots)
    live_rows = (slots % slot_count < limits).astype(jnp.bfloat16)[:, None]
    left_live = left_cols * live_rows
    right_live = right_cols * live_rows
    feature_dims = (((1,), (1,)), ((), ()))
    hidden_part = lax.dot_general(
        tokens, left_live, feature_dims, preferred_element_type=jnp.float32
    )
    back_part = lax.dot_general(
        cotangent, right_live, feature_dims, preferred_element_type=jnp.float32
    )
    hidden, back_hidden = lax.psum((hidden_part, back_part), "tensor")
    hidden = hidden.astype(jnp.bfloat16)
    back_hidden = back_hidden.astype(jnp.bfloat16)
    grad_scale = 1.0 / math.sqrt(tokens.shape[0] * lax.axis_size("dp"))
    token_dims = (((0,), (0,)), ((), ()))
    right_local = (
        lax.dot_general(hidden, cotangent, token_dims, preferred_element_type=jnp.float32)
        * grad_scale
    )
    left_local = (
        lax.dot_general(back_hidden, tokens, token_dims, preferred_element_type=jnp.float32)
        * grad_scale
    )
    token_grad = jnp.dot(back_hidden, left_live, preferred_element_type=jnp.float32).astype(
        jnp.bfloat16
    )
    left_grad, right_grad = settle_both(left_local, right_local)
    return (token_grad, left_grad, right_grad)


def solution(mesh):
    placed = (P("dp", "tensor"), P("dp", "tensor"), P("tensor", None), P("tensor", None), P())
    return jax.shard_map(
        local,
        mesh=mesh,
        in_specs=placed,
        out_specs=(P("dp", "tensor"), P("tensor", None, "dp", None), P("tensor", None, "dp", None)),
        check_vma=False,
    )
```

profile of v0, /device:TPU:16, one launch (start us, length us, event | category | flops | bytes accessed | tf_op | source)
XLA Modules:
  0.0 882.0 jit_solution(2963327781029973824)
XLA Ops:
  7.2 0.0 copy-start
  7.2 2.2 copy.25
  9.4 9.1 %all-to-all-start = ((bf16[24,8,2048]{2,0,1:T(8,128)(2,1)}), bf16[24,8,2048]{2,0,1:T(8,128)(2,1)S(1)}, u32[]{:S(2)}, u32[]{:S(2)}) async-start(bf16[24,8,2048]{2,0,1:T(8,128)(2,1)} %bitcast.43), calls=%async_computation | async-start | bytes 1572864 | tf_op jit(solution)/shard_map/all_to_all | solution.py:37
  18.6 1.0 copy.24
  19.6 19.1 %all-to-all-done = bf16[24,8,2048]{2,0,1:T(8,128)(2,1)S(1)} async-done(((bf16[24,8,2048]{2,0,1:T(8,128)(2,1)}), bf16[24,8,2048]{2,0,1:T(8,128)(2,1)S(1)}, u32[]{:S(2)}, u32[]{:S(2)}) %all-to-all-start) | async-done | bytes 786464 | tf_op jit(solution)/shard_map/all_to_all | solution.py:37
  38.6 5.6 all-to-all-start.1
  44.2 0.0 copy-done.3
  44.2 0.7 fusion.3
  44.9 0.1 add_bitcast_fusion
  45.0 5.2 compare_convert_fusion
  50.2 12.2 %all-to-all-done.1 = bf16[24,8,2048]{2,0,1:T(8,128)(2,1)} async-done(((bf16[24,8,2048]{2,0,1:T(8,128)(2,1)}), bf16[24,8,2048]{2,0,1:T(8,128)(2,1)}, u32[]{:S(2)}, u32[]{:S(2)}) %all-to-all-start.1) | async-done | bytes 786464 | tf_op jit(solution)/shard_map/all_to_all | solution.py:36
  62.4 1.4 bitcast_multiply_fusion.1
  63.7 0.0 copy-start.1
  63.8 0.7 convolution_bitcast_fusion
  64.4 0.7 copy-done.1
  65.1 0.7 convolution_bitcast_fusion.1
  65.8 36.2 %all-reduce.6 = (bf16[384,192]{0,1:T(8,128)(2,1)S(1)}, bf16[384,192]{0,1:T(8,128)(2,1)S(1)}) all-reduce(f32[384,192]{0,1:T(8,128)S(1)} %convolution_bitcast_fusion.1, f32[384,192]{0,1:T(8,128)S(1)} %convolution_bitcast_fusion), channel_id=1, replica_groups=mesh['dp'=64,'tensor'=8] {'tensor'}, use_global_device_ids=true, to_apply=%region_0.1 | all-reduce | flops 147456 | bytes 884736 | tf_op jit(solution)/shard_map/psum | solution.py:51
  102.1 1.7 convolution_multiply_fusion.1
  103.8 9.1 %all-to-all-start.2 = ((f32[8,24,2048]{2,1,0:T(8,128)}), f32[8,24,2048]{2,1,0:T(8,128)}, u32[]{:S(2)}, u32[]{:S(2)}) async-start(f32[8,24,2048]{2,1,0:T(8,128)} %bitcast.45), calls=%async_computation.2 | async-start | bytes 3145728 | tf_op jit(solution)/shard_map/all_to_all | solution.py:22
  112.9 3.2 convolution_multiply_fusion
  116.1 33.5 %all-to-all-done.2 = f32[8,24,2048]{2,1,0:T(8,128)} async-done(((f32[8,24,2048]{2,1,0:T(8,128)}), f32[8,24,2048]{2,1,0:T(8,128)}, u32[]{:S(2)}, u32[]{:S(2)}) %all-to-all-start.2) | async-done | bytes 1572896 | tf_op jit(solution)/shard_map/all_to_all | solution.py:22
  149.7 5.9 all-to-all-start.3
  155.6 0.0 all-reduce.5.cloned.1.call-start
  155.6 3.5 copy.18
  159.0 5.1 reshape.82
  164.2 24.5 %all-to-all-done.3 = f32[8,24,2048]{2,1,0:T(8,128)} async-done(((f32[8,24,2048]{2,1,0:T(8,128)}), f32[8,24,2048]{2,1,0:T(8,128)}, u32[]{:S(2)}, u32[]{:S(2)}) %all-to-all-start.3) | async-done | bytes 1572896 | tf_op jit(solution)/shard_map/all_to_all | solution.py:23
  188.7 3.5 copy.19
  192.2 5.2 reshape.83
  197.4 0.0 all-reduce.5.cloned.1.call-update
  197.4 1.7 convolution_convert_fusion
  199.1 673.8 %all-reduce.5.cloned.1.call-done = (f32[24,8,64,32]{3,2,1,0:T(8,128)}, f32[24,8,64,32]{3,2,1,0:T(8,128)}) async-done(((f32[24,8,64,32]{3,2,1,0:T(8,128)}, f32[24,8,64,32]{3,2,1,0:T(8,128)}), (f32[24,8,64,32]{3,2,1,0:T(8,128)}, f32[24,8,64,32]{3,2,1,0:T(8,128)})) %all-reduce.5.cloned.1.call-update) | async-done | bytes 3145744 | tf_op jit(solution)/shard_map/psum | solution.py:27
  872.9 2.2 constant_dynamic-slice_fusion
  (7 shorter events, 0.0 us)
Async XLA Ops:
  7.2 56.6 %copy-start = (bf16[384,2048]{1,0:T(8,128)(2,1)S(1)}, bf16[384,2048]{1,0:T(8,128)(2,1)}, u32[]{:S(2)}) copy-start(bf16[384,2048]{1,0:T(8,128)(2,1)} %param.7) | copy-start | bytes 4718596
  7.2 11.4 %copy-start.2 = (bf16[24,16384]{1,0:T(8,128)(2,1)S(1)}, bf16[24,16384]{1,0:T(8,128)(2,1)}, u32[]{:S(2)}) copy-start(bf16[24,16384]{1,0:T(8,128)(2,1)} %param.9) | copy-start | bytes 2359300
  9.4 29.2 %all-to-all-start = ((bf16[24,8,2048]{2,0,1:T(8,128)(2,1)}), bf16[24,8,2048]{2,0,1:T(8,128)(2,1)S(1)}, u32[]{:S(2)}, u32[]{:S(2)}) async-start(bf16[24,8,2048]{2,0,1:T(8,128)(2,1)} %bitcast.43), calls=%async_computation | async-start | bytes 1572864 | tf_op jit(solution)/shard_map/all_to_all | solution.py:37
  18.6 25.7 %copy-start.3 = (s32[8]{0:T(128)S(1)}, s32[8]{0:T(128)}, u32[]{:S(2)}) copy-start(s32[8]{0:T(128)} %param.11) | copy-start | bytes 100
  18.6 26.3 %copy-start.4 = (s32[2,128]{1,0:T(2,128)S(1)}, s32[2,128]{1,0:T(2,128)}, u32[]{:S(2)}) copy-start(s32[2,128]{1,0:T(2,128)} %constant.92.clone.1) | copy-start | bytes 3076
  38.6 23.7 %all-to-all-start.1 = ((bf16[24,8,2048]{2,0,1:T(8,128)(2,1)}), bf16[24,8,2048]{2,0,1:T(8,128)(2,1)}, u32[]{:S(2)}, u32[]{:S(2)}) async-start(bf16[24,8,2048]{2,0,1:T(8,128)(2,1)} %bitcast.42), calls=%async_computation.1 | async-start | bytes 1572864 | tf_op jit(solution)/shard_map/all_to_all | solution.py:36
  63.7 1.4 copy-start.1
  103.8 45.9 %all-to-all-start.2 = ((f32[8,24,2048]{2,1,0:T(8,128)}), f32[8,24,2048]{2,1,0:T(8,128)}, u32[]{:S(2)}, u32[]{:S(2)}) async-start(f32[8,24,2048]{2,1,0:T(8,128)} %bitcast.45), calls=%async_computation.2 | async-start | bytes 3145728 | tf_op jit(solution)/shard_map/all_to_all | solution.py:22
  149.7 39.0 %all-to-all-start.3 = ((f32[8,24,2048]{2,1,0:T(8,128)}), f32[8,24,2048]{2,1,0:T(8,128)}, u32[]{:S(2)}, u32[]{:S(2)}) async-start(f32[8,24,2048]{2,1,0:T(8,128)} %bitcast.44), calls=%async_computation.3 | async-start | bytes 3145728 | tf_op jit(solution)/shard_map/all_to_all | solution.py:23
  155.6 717.4 %all-reduce.5.cloned.1.call-start = ((), (), s32[]{:S(2)}) async-start(), calls=%async_computation.4 | async-start | bytes 25165824 | tf_op jit(solution)/shard_map/psum | solution.py:27
Sparse Core Ops, SparseCore 0:
  197.5 675.3 all-reduce.4
where the time goes:
time: 883 us; the launch traced here: 882 us
  waiting for transfers between devices  763 us (86%)
  blocking collectives  36.2 us (4%)
  starting transfers between devices  29.7 us (3%)
  local copies, waits for them, and re-layouts  24.1 us (3%)
  between operations  14.1 us (2%)
    psum x1, waiting for transfers between devices, settle_both(): left_sum, right_sum = lax.psum((left_home, right_home), 'dp')  674 us
    psum x1, blocking collectives, local(): hidden, back_hidden = lax.psum((hidden_part, back_part), 'tensor')  36.2 us
    all_to_all x1, waiting for transfers between devices, settle_both(): lax.all_to_all(left_cols, 'tensor', split_axis=0, concat_axis=1, tiled=True)  33.5 us
    all_to_all x1, waiting for transfers between devices, settle_both(): lax.all_to_all(right_cols, 'tensor', split_axis=0, concat_axis=1, tiled=T...  24.5 us
    all_to_all x1, waiting for transfers between devices, local(): lax.all_to_all(right_factor, 'tensor', split_axis=1, concat_axis=0, tiled...  19.1 us
  transfers between devices with their start and end apart: 5, of which 5 were waited for; matrix products, arithmetic and copies ran while one was open for 2% of the time, Pallas kernels for 0%

commit v1 on v0

v1 whole, which is shorter than its diff:
```python
import math

import jax
import jax.numpy as jnp
from jax import lax
from jax.sharding import PartitionSpec as P


def local(tokens, cotangent, left_factor, right_factor, panel_rank):
    slot_count = left_factor.shape[0]
    groups = lax.axis_size("tensor")
    width = lax.axis_size("dp")
    all_slots = slot_count * groups
    features = tokens.shape[1]
    block = features // width
    factors = jnp.concatenate((left_factor, right_factor), axis=0)
    cols = lax.all_to_all(factors, "tensor", split_axis=1, concat_axis=0, tiled=True)
    cols = cols.reshape(groups, 2, slot_count, features)
    limits = panel_rank.reshape(groups, 1, 1, 1)
    slots = lax.broadcasted_iota(jnp.int32, (1, 1, slot_count, 1), 2)
    live = cols * (slots < limits).astype(jnp.bfloat16)
    left_live = live[:, 0].reshape(all_slots, features)
    right_live = live[:, 1].reshape(all_slots, features)
    feature_dims = (((1,), (1,)), ((), ()))
    hidden_part = lax.dot_general(
        tokens, left_live, feature_dims, preferred_element_type=jnp.float32
    )
    back_part = lax.dot_general(
        cotangent, right_live, feature_dims, preferred_element_type=jnp.float32
    )
    hidden, back_hidden = lax.psum((hidden_part, back_part), "tensor")
    hidden = hidden.astype(jnp.bfloat16)
    back_hidden = back_hidden.astype(jnp.bfloat16)
    grad_scale = 1.0 / math.sqrt(tokens.shape[0] * width)
    token_dims = (((0,), (0,)), ((), ()))
    left_t = lax.dot_general(tokens, back_hidden, token_dims, preferred_element_type=jnp.float32)
    right_t = lax.dot_general(cotangent, hidden, token_dims, preferred_element_type=jnp.float32)
    both = jnp.concatenate((left_t, right_t), axis=1).astype(jnp.bfloat16)
    both = both.reshape(width, block, 2 * all_slots)
    swapped = lax.all_to_all(both, "dp", split_axis=0, concat_axis=0, tiled=True)
    mine = swapped.astype(jnp.float32).sum(0) * grad_scale
    mine = mine.reshape(block, 2, groups, slot_count).transpose(2, 1, 3, 0)
    home = lax.all_to_all(mine, "tensor", split_axis=0, concat_axis=0, tiled=True)
    home = home.transpose(1, 2, 0, 3)[:, :, :, None, :]
    token_grad = jnp.dot(back_hidden, left_live, preferred_element_type=jnp.float32).astype(
        jnp.bfloat16
    )
    return (token_grad, home[0], home[1])


def solution(mesh):
    placed = (P("dp", "tensor"), P("dp", "tensor"), P("tensor", None), P("tensor", None), P())
    return jax.shard_map(
        local,
        mesh=mesh,
        in_specs=placed,
        out_specs=(P("dp", "tensor"), P("tensor", None, "dp", None), P("tensor", None, "dp", None)),
        check_vma=False,
    )
```

time: 883 us -> 167 us (0.19)
  the two profiles are of different devices: /device:TPU:16 before, /device:TPU:1 now
where the time goes in v1:
time: 167 us
  blocking collectives  85.2 us (51%)
  waiting for transfers between devices  43.1 us (26%)
  starting transfers between devices  16.9 us (10%)
  local copies, waits for them, and re-layouts  8.95 us (5%)
  matrix products  7.49 us (4%)
  other arithmetic  4.7 us (3%)
    all_to_all x1, blocking collectives, local(): lax.all_to_all(both, 'dp', split_axis=0, concat_axis=0, tiled=True)  54 us
    all_to_all x1, waiting for transfers between devices, local(): lax.all_to_all(factors, 'tensor', split_axis=1, concat_axis=0, tiled=True)  37.5 us
    psum x1, blocking collectives, local(): hidden, back_hidden = lax.psum((hidden_part, back_part), 'tensor')  31.1 us
    all_to_all x1, starting transfers between devices, local(): lax.all_to_all(factors, 'tensor', split_axis=1, concat_axis=0, tiled=True)  10.5 us
    all_to_all x1, starting transfers between devices, local(): lax.all_to_all(mine, 'tensor', split_axis=0, concat_axis=0, tiled=True)  6.41 us
    all_to_all x1, waiting for transfers between devices, local(): lax.all_to_all(mine, 'tensor', split_axis=0, concat_axis=0, tiled=True)  5.59 us
  transfers between devices with their start and end apart: 2, of which 2 were waited for; matrix products, arithmetic and copies ran while one was open for 1% of the time, Pallas kernels for 0%

profile of v1, /device:TPU:1, one launch (start us, length us, event | category | flops | bytes accessed | tf_op | source)
XLA Modules:
  0.0 167.0 jit_solution(13050618455040787968)
XLA Ops:
  0.6 0.0 copy-start
  0.6 1.6 pad_maximum_fusion
  2.2 1.2 copy.29
  3.5 10.5 %all-to-all-start = ((bf16[48,8,2048]{2,0,1:T(8,128)(2,1)}), bf16[48,8,2048]{2,0,1:T(8,128)(2,1)S(1)}, u32[]{:S(2)}, u32[]{:S(2)}) async-start(bf16[48,8,2048]{2,0,1:T(8,128)(2,1)} %bitcast.34), calls=%async_computation | async-start | bytes 3145728 | tf_op jit(solution)/shard_map/all_to_all | solution.py:17
  13.9 0.0 copy-done.2
  13.9 0.1 fusion.5
  14.0 37.5 %all-to-all-done = bf16[48,8,2048]{2,0,1:T(8,128)(2,1)S(1)} async-done(((bf16[48,8,2048]{2,0,1:T(8,128)(2,1)}), bf16[48,8,2048]{2,0,1:T(8,128)(2,1)S(1)}, u32[]{:S(2)}, u32[]{:S(2)}) %all-to-all-start) | async-done | bytes 1572896 | tf_op jit(solution)/shard_map/all_to_all | solution.py:17
  51.6 0.2 broadcast_multiply_fusion
  51.7 0.1 fusion.6
  51.9 0.0 copy-start.1
  51.9 0.7 convolution_bitcast_fusion
  52.6 0.7 copy-done.1
  53.3 0.7 convolution_bitcast_fusion.1
  54.0 31.1 %all-reduce.2 = (bf16[384,192]{0,1:T(8,128)(2,1)S(1)}, bf16[384,192]{0,1:T(8,128)(2,1)}) all-reduce(f32[384,192]{0,1:T(8,128)S(1)} %convolution_bitcast_fusion.1, f32[384,192]{0,1:T(8,128)S(1)} %convolution_bitcast_fusion), channel_id=1, replica_groups=mesh['dp'=64,'tensor'=8] {'tensor'}, use_global_device_ids=true, to_apply=%region_0.0 | all-reduce | flops 147456 | bytes 884736 | tf_op jit(solution)/shard_map/psum | solution.py:31
  85.1 1.5 fusion
  86.5 1.4 copy.22
  88.0 3.0 %fusion.1 = bf16[2048,192]{0,1:T(8,128)(2,1)} fusion(bf16[384,2048]{1,0:T(8,128)(2,1)} %param.6, bf16[384,192]{0,1:T(8,128)(2,1)} %get-tuple-element.16), kind=kOutput, calls=%fused_computation.5 | convolution fusion | flops 302383104 | bytes 2506752 | tf_op jit(solution)/shard_map/dot_general | solution.py:37
  90.9 2.2 %copy.23 = bf16[2048,192]{1,0:T(8,128)(2,1)} copy(bf16[2048,192]{0,1:T(8,128)(2,1)} %fusion.1) | data formatting | bytes 1572864 | tf_op jit(solution)/shard_map/dot_general | solution.py:37
  93.1 1.9 %pad_maximum_fusion.1 = bf16[64,32,384]{2,1,0:T(8,128)(2,1)S(1)} fusion(bf16[64,32,192]{2,1,0:T(8,128)(2,1)} %bitcast.40, bf16[64,32,192]{2,1,0:T(8,128)(2,1)S(1)} %bitcast.39), kind=kLoop, calls=%fused_computation.8 | loop fusion | flops 3145728 | bytes 3145728 | tf_op jit(solution)/shard_map/concatenate | solution.py:38
  95.0 54.0 %all_to_all.26 = bf16[64,32,384]{2,1,0:T(8,128)(2,1)S(1)} all-to-all(bf16[64,32,384]{2,1,0:T(8,128)(2,1)S(1)} %pad_maximum_fusion.1), channel_id=1, replica_groups=mesh['dp'=64,'tensor'=8] {'dp'}, dimensions={0} | all-to-all | bytes 3145728 | tf_op jit(solution)/shard_map/all_to_all | solution.py:40
  149.1 0.2 convert_reduce_fusion
  149.3 0.2 mul.22
  149.5 0.2 copy.24
  149.6 0.8 reshape.54
  150.4 6.4 %all-to-all-start.2 = ((f32[8,1,1536]{2,1,0:T(1,128)}), f32[8,1,1536]{2,1,0:T(1,128)S(1)}, u32[]{:S(2)}, u32[]{:S(2)}) async-start(f32[8,1,1536]{2,1,0:T(1,128)} %reshape.54), calls=%async_computation.2 | async-start | bytes 98304 | tf_op jit(solution)/shard_map/all_to_all | solution.py:43
  156.8 1.7 %convolution_convert_fusion = bf16[384,2048]{1,0:T(8,128)(2,1)} fusion(bf16[192,2048]{1,0:T(8,128)(2,1)S(1)} %bitcast.36, bf16[384,192]{0,1:T(8,128)(2,1)S(1)} %get-tuple-element.15), kind=kOutput, calls=%fused_computation.1 | convolution fusion | flops 302776320 | bytes 2506752 | tf_op jit(solution)/shard_map/dot_general | solution.py:45
  158.6 5.6 %all-to-all-done.2 = f32[8,1,1536]{2,1,0:T(1,128)S(1)} async-done(((f32[8,1,1536]{2,1,0:T(1,128)}), f32[8,1,1536]{2,1,0:T(1,128)S(1)}, u32[]{:S(2)}, u32[]{:S(2)}) %all-to-all-start.2) | async-done | bytes 49184 | tf_op jit(solution)/shard_map/all_to_all | solution.py:43
  164.2 0.5 broadcast.20
  164.7 0.8 reduce
  165.4 0.1 reshape.55
  165.6 0.7 copy.25
  166.3 0.7 copy.26
  (4 shorter events, 0.0 us)
Async XLA Ops:
  0.6 51.3 %copy-start = (bf16[384,2048]{1,0:T(8,128)(2,1)S(1)}, bf16[384,2048]{1,0:T(8,128)(2,1)}, u32[]{:S(2)}) copy-start(bf16[384,2048]{1,0:T(8,128)(2,1)} %param.5) | copy-start | bytes 4718596
  3.5 10.5 %copy-start.2 = (s32[8]{0:T(128)S(1)}, s32[8]{0:T(128)}, u32[]{:S(2)}) copy-start(s32[8]{0:T(128)} %param.9) | copy-start | bytes 100
  3.5 48.1 %all-to-all-start = ((bf16[48,8,2048]{2,0,1:T(8,128)(2,1)}), bf16[48,8,2048]{2,0,1:T(8,128)(2,1)S(1)}, u32[]{:S(2)}, u32[]{:S(2)}) async-start(bf16[48,8,2048]{2,0,1:T(8,128)(2,1)} %bitcast.34), calls=%async_computation | async-start | bytes 3145728 | tf_op jit(solution)/shard_map/all_to_all | solution.py:17
  51.9 1.4 copy-start.1
  150.4 13.7 %all-to-all-start.2 = ((f32[8,1,1536]{2,1,0:T(1,128)}), f32[8,1,1536]{2,1,0:T(1,128)S(1)}, u32[]{:S(2)}, u32[]{:S(2)}) async-start(f32[8,1,1536]{2,1,0:T(1,128)} %reshape.54), calls=%async_computation.2 | async-start | bytes 98304 | tf_op jit(solution)/shard_map/all_to_all | solution.py:43

commit v2 on v1

v2 whole, which is shorter than its diff:
```python
import functools
import math

import jax
import jax.numpy as jnp
from jax import lax
from jax.experimental import pallas as pl
from jax.experimental.pallas import tpu as pltpu
from jax.sharding import PartitionSpec as P

LANES = 128
BF16 = jnp.bfloat16
F32 = jnp.float32


def over_rows(a, b):
    return lax.dot_general(a, b, (((0,), (0,)), ((), ())), preferred_element_type=F32)


def over_lanes(a, b):
    return lax.dot_general(a, b, (((1,), (1,)), ((), ())), preferred_element_type=F32)


def kernel(
    nz, nw, nt, kc, scale,
    rank_ref, facs, tok_hbm, cot_hbm,
    tg_hbm, out_ref,
    tok, cot, raw, pick, spread, rows, hid32, hid16, pair_in, pair, quad_in, hidden,
    part, from_w, from_z, sum_w, sum_z, last_z, last_w, piece, home, tgrad,
    loc, a1s, a1r, aws, awr, azs, azr, b1, b2, b3, b4, cws, cwr, czs, czr, dzs, dzr, dws, dwr, es, er,
):
    d = lax.axis_index("dp")
    t = lax.axis_index("tensor")
    z, w = lax.div(d, nw), lax.rem(d, nw)
    yh, core = lax.div(t, 2), lax.rem(t, 2)
    nh = nt // 2
    k2 = 2 * kc
    tokens, features = tok.shape
    twice = raw.shape[2]
    slots = twice // 2
    half = part.shape[3]
    nq = part.shape[0]
    nwq = sum_w.shape[0]
    split = (3 * k2 // 8) // 16 * 16

    def at_t(k):
        return (d, lax.rem(t + k, nt))

    def at_w(k):
        return (z * nw + lax.rem(w + k, nw), t)

    def at_z(k):
        return (lax.rem(z + k, nz) * nw + w, t)

    def at_h(k):
        return (d, lax.rem(yh + k, nh) * 2 + core)

    mate = (d, t + 1 - 2 * core)

    def send(src, dst, ssem, rsem, dev):
        copy = pltpu.make_async_remote_copy(
            src_ref=src, dst_ref=dst, send_sem=ssem, recv_sem=rsem,
            device_id=dev, device_id_type=pl.DeviceIdType.MESH,
        )
        copy.start()
        return copy

    sent = []
    tiles = (w, nw + w, nw + z)

    def cut(owner, tile):
        return facs.at[:, pl.ds(pl.multiple_of(owner * features + tile * LANES, LANES), LANES)]

    local = [pltpu.make_async_copy(cut(t, tiles[i]), raw.at[i, t], loc.at[i]) for i in range(3)]
    load_cot = pltpu.make_async_copy(cot_hbm, cot, loc.at[3])
    load_tok = pltpu.make_async_copy(tok_hbm, tok, loc.at[4])
    for copy in local:
        copy.start()
    load_cot.start()
    load_tok.start()

    barrier = pltpu.get_barrier_semaphore()
    peers = [at_t(k) for k in range(1, nt)] + [at_w(k) for k in range(1, nw)] + [at_z(k) for k in range(1, nz)]
    for peer in peers:
        pl.semaphore_signal(barrier, inc=1, device_id=peer, device_id_type=pl.DeviceIdType.MESH)
    pl.semaphore_wait(barrier, len(peers))

    first = []
    for i in (2, 0, 1):
        for k in range(1, nt):
            dev = at_t(k)
            first.append(send(cut(dev[1], tiles[i]), raw.at[i, t], a1s.at[k - 1, i], a1r.at[k - 1, i], dev))
    sent += first

    column = lax.broadcasted_iota(jnp.int32, (8, nt * twice), 1)
    slot_c = column
    base_c = jnp.zeros((8, nt * twice), jnp.int32)
    rank_c = jnp.zeros((8, nt * twice), jnp.int32)
    slot_r = lax.broadcasted_iota(jnp.int32, (nt * slots, kc), 0)
    base_r = jnp.zeros((nt * slots, kc), jnp.int32)
    rank_r = jnp.zeros((nt * slots, kc), jnp.int32)
    base = jnp.int32(0)
    for p in range(nt):
        inside = column >= p * twice
        slot_c = jnp.where(inside, column - p * twice, slot_c)
        base_c = jnp.where(inside, base, base_c)
        rank_c = jnp.where(inside, rank_ref[p], rank_c)
        inside = slot_r >= p * slots
        base_r = jnp.where(inside, base - p * slots, base_r)
        rank_r = jnp.where(inside, rank_ref[p] + p * slots, rank_r)
        base = base + rank_ref[p]
    row = lax.broadcasted_iota(jnp.int32, (kc, nt * twice), 0)
    place = jnp.where(slot_c < rank_c, base_c + slot_c, -1)[0:1]
    pick[0:kc, :] = (row == place).astype(F32).astype(BF16)
    slot_c = slot_c - slots
    place = jnp.where((slot_c >= 0) & (slot_c < rank_c), base_c + slot_c, -1)[0:1]
    pick[kc:k2, :] = (row == place).astype(F32).astype(BF16)
    col = lax.broadcasted_iota(jnp.int32, (nt * slots, kc), 1)
    spread[...] = ((col == slot_r + base_r) & (slot_r < rank_r)).astype(F32).astype(BF16)

    for copy in local:
        copy.wait()
    second = []

    def picked(i, low, high):
        return jnp.dot(
            pick[low:high, :], raw[i].reshape(nt * twice, LANES), preferred_element_type=F32
        ).astype(BF16)

    for copy in first[: nt - 1]:
        copy.wait_recv()
    rows[nw + z, split:k2, :] = picked(2, split, k2)
    for k in range(1, nz):
        ref = rows.at[nw + z, split:k2, :]
        second.append(send(ref, ref, azs.at[k - 1], azr.at[k - 1], at_z(k)))
    for copy in first[nt - 1 : 2 * (nt - 1)]:
        copy.wait_recv()
    rows[w, :, :] = picked(0, 0, k2)
    for k in range(1, nw):
        ref = rows.at[w]
        second.append(send(ref, ref, aws.at[k - 1, 0], awr.at[k - 1, 0], at_w(k)))
    for copy in first[2 * (nt - 1) :]:
        copy.wait_recv()
    rows[nw + w, 0:split, :] = picked(1, 0, split)
    for k in range(1, nw):
        ref = rows.at[nw + w, 0:split, :]
        second.append(send(ref, ref, aws.at[k - 1, 1], awr.at[k - 1, 1], at_w(k)))
    sent += second
    load_cot.wait()
    load_tok.wait()
    for copy in second:
        copy.wait_recv()

    left = jnp.concatenate([rows[i, 0:kc, :] for i in range(nw + nz)], axis=1)
    right = jnp.concatenate([rows[i, kc:k2, :] for i in range(nw + nz)], axis=1)
    share = tokens // nt
    hid32[:, :, 0:kc] = over_lanes(tok[...], left).reshape(nt, share, kc)
    hid32[:, :, kc:k2] = over_lanes(cot[...], right).reshape(nt, share, kc)
    hid16[...] = hid32[...].astype(BF16)
    copy = send(hid16.at[pl.ds((1 - core) * nh, nh)], pair_in, b1.at[0], b1.at[1], mate)
    sent.append(copy)
    copy.wait_recv()
    mine = hid32[pl.ds(core * nh, nh)] + pair_in[...].astype(F32)
    pair[...] = mine.astype(BF16)
    swaps = []
    for k in range(1, nh):
        to = lax.rem(yh + k, nh)
        swaps.append(send(pair.at[to], quad_in.at[k - 1], b2.at[0, k - 1], b2.at[1, k - 1], at_h(k)))
    sent += swaps
    total = hid32[core * nh + yh] + pair_in[yh].astype(F32)
    for k in range(1, nh):
        swaps[k - 1].wait_recv()
        total = total + quad_in[k - 1].astype(F32)
    own = core * nh + yh
    hidden[own] = total.astype(BF16)
    shares = []
    for k in range(1, nh):
        ref = hidden.at[own]
        shares.append(send(ref, ref, b3.at[0, k - 1], b3.at[1, k - 1], at_h(k)))
    relay = [send(hidden.at[own], hidden.at[own], b4.at[0, 0], b4.at[1, 0], mate)]
    for k in range(1, nh):
        shares[k - 1].wait_recv()
        ref = hidden.at[core * nh + lax.rem(yh + nh - k, nh)]
        relay.append(send(ref, ref, b4.at[0, k], b4.at[1, k], mate))
    for copy in relay:
        copy.wait_recv()
    sent += shares + relay

    zone = features // nz
    tiles_k = kc // LANES

    def outer(array, columns, slab):
        for zb in range(nz):
            full = over_rows(array[:, zb * zone : (zb + 1) * zone], columns).astype(BF16)
            full = full.reshape(nw, 2, half, kc)
            for j in range(tiles_k):
                for h in range(2):
                    part[slab + 2 * j + h, zb] = full[:, h, :, j * LANES : (j + 1) * LANES]

    back = hidden[:, :, kc:k2].reshape(tokens, kc)
    outer(tok, back, 0)
    third_w, third_z = [], []
    for k in range(1, nw):
        to = lax.rem(w + k, nw)
        third_w.append(
            send(part.at[0 : nq // 2, :, to], from_w.at[k - 1, 0 : nq // 2], cws.at[k - 1, 0], cwr.at[k - 1, 0], at_w(k))
        )
    outer(cot, hidden[:, :, 0:kc].reshape(tokens, kc), nq // 2)
    for k in range(1, nz):
        to = lax.rem(z + k, nz)
        third_z.append(send(part.at[nwq:nq, to], from_z.at[k - 1], czs.at[k - 1], czr.at[k - 1], at_z(k)))
    for k in range(1, nw):
        to = lax.rem(w + k, nw)
        third_w.append(
            send(part.at[nq // 2 : nwq, :, to], from_w.at[k - 1, nq // 2 : nwq], cws.at[k - 1, 1], cwr.at[k - 1, 1], at_w(k))
        )
    sent += third_w + third_z

    for i in range(0, nw + nz, 2):
        both = jnp.concatenate([rows[i, 0:kc, :], rows[i + 1, 0:kc, :]], axis=1)
        tgrad[:, i * LANES : (i + 2) * LANES] = jnp.dot(back, both, preferred_element_type=F32).astype(BF16)
    store_tg = pltpu.make_async_copy(tgrad, tg_hbm, loc.at[5])
    store_tg.start()

    fourth = []
    for copy in third_z:
        copy.wait_recv()
    total = part[nwq:nq, z].astype(F32)
    for k in range(1, nz):
        total = total + from_z[k - 1].astype(F32)
    sum_z[...] = total.astype(BF16)
    for k in range(1, nw):
        to = lax.rem(w + k, nw)
        fourth.append(send(sum_z.at[:, to], last_w.at[k - 1], dws.at[k - 1], dwr.at[k - 1], at_w(k)))
    for copy in third_w:
        copy.wait_recv()
    for q in range(nwq):
        total = part[q, :, w].astype(F32)
        for k in range(1, nw):
            total = total + from_w[k - 1, q].astype(F32)
        sum_w[q] = total.astype(BF16)
    for k in range(1, nz):
        to = lax.rem(z + k, nz)
        fourth.append(send(sum_w.at[:, to], last_z.at[k - 1], dzs.at[k - 1], dzr.at[k - 1], at_z(k)))
    sent += fourth
    for copy in fourth:
        copy.wait_recv()
    sum_a = sum_w[:, z].astype(F32)
    for k in range(1, nz):
        sum_a = sum_a + last_z[k - 1].astype(F32)
    sum_b = sum_z[:, w].astype(F32)
    for k in range(1, nw):
        sum_b = sum_b + last_w[k - 1].astype(F32)
    slabs = [sum_a[q] * scale for q in range(nwq)] + [sum_b[q] * scale for q in range(nq - nwq)]

    def side(first_slab):
        return jnp.concatenate(
            [jnp.concatenate([slabs[first_slab + 2 * j], slabs[first_slab + 2 * j + 1]], axis=0) for j in range(tiles_k)],
            axis=1,
        )

    final = [side(0), side(nq // 2)]
    spare = piece.shape[2] - 4 * half
    if spare:
        final.append(jnp.zeros((spare, kc), F32))
    final = jnp.concatenate(final, axis=0)
    high = final.astype(BF16)
    rest = final - high.astype(F32)
    middle = rest.astype(BF16)
    low = (rest - middle.astype(F32)).astype(BF16)
    chosen = spread[...]
    placed = over_lanes(chosen, high) + over_lanes(chosen, middle) + over_lanes(chosen, low)
    piece[...] = placed.reshape(nt, slots, piece.shape[2])
    fifth = []
    for k in range(1, nt):
        to = lax.rem(t + k, nt)
        fifth.append(send(piece.at[to], home.at[t], es.at[k - 1], er.at[k - 1], at_t(k)))
    home[t] = piece[t]
    for copy in fifth:
        copy.wait_recv()
    out_ref[...] = home[...]
    sent += fifth
    for copy in sent:
        copy.wait_send()
    store_tg.wait()


def fused(sizes, kc, ident, panel_rank, facs, tokens, cotangent):
    nz, nw, nt = sizes
    count, features = tokens.shape
    twice = facs.shape[0]
    slots = twice // 2
    k2 = 2 * kc
    nq = 2 * k2 // LANES
    nwq = 3 * nq // 4
    half = features // (nz * nw * 2)
    wide = max(LANES, 4 * half)
    share = count // nt
    nh = nt // 2
    scale = 1.0 / math.sqrt(count * nz * nw)
    dma = pltpu.SemaphoreType.DMA
    vmem = pltpu.VMEM
    scratch = [
        vmem((count, features), BF16),
        vmem((count, features), BF16),
        vmem((3, nt, twice, LANES), BF16),
        vmem((k2, nt * twice), BF16),
        vmem((nt * slots, kc), BF16),
        vmem((nw + nz, k2, LANES), BF16),
        vmem((nt, share, k2), F32),
        vmem((nt, share, k2), BF16),
        vmem((nh, share, k2), BF16),
        vmem((nh, share, k2), BF16),
        vmem((nh - 1, share, k2), BF16),
        vmem((nt, share, k2), BF16),
        vmem((nq, nz, nw, half, LANES), BF16),
        vmem((nw - 1, nwq, nz, half, LANES), BF16),
        vmem((nz - 1, nq - nwq, nw, half, LANES), BF16),
        vmem((nwq, nz, half, LANES), BF16),
        vmem((nq - nwq, nw, half, LANES), BF16),
        vmem((nz - 1, nwq, half, LANES), BF16),
        vmem((nw - 1, nq - nwq, half, LANES), BF16),
        vmem((nt, slots, wide), F32),
        vmem((nt, slots, wide), F32),
        vmem((count, features), BF16),
        dma((6,)),
        dma((nt - 1, 3)),
        dma((nt - 1, 3)),
        dma((nw - 1, 2)),
        dma((nw - 1, 2)),
        dma((nz - 1,)),
        dma((nz - 1,)),
        dma((2,)),
        dma((2, nh - 1)),
        dma((2, nh - 1)),
        dma((2, nh)),
        dma((nw - 1, 2)),
        dma((nw - 1, 2)),
        dma((nz - 1,)),
        dma((nz - 1,)),
        dma((nz - 1,)),
        dma((nz - 1,)),
        dma((nw - 1,)),
        dma((nw - 1,)),
        dma((nt - 1,)),
        dma((nt - 1,)),
    ]
    anywhere = pl.BlockSpec(memory_space=pl.ANY)
    return pl.pallas_call(
        functools.partial(kernel, nz, nw, nt, kc, scale),
        out_shape=(
            jax.ShapeDtypeStruct((count, features), BF16),
            jax.ShapeDtypeStruct((nt, slots, wide), F32),
        ),
        in_specs=[pl.BlockSpec(memory_space=pltpu.SMEM), anywhere, anywhere, anywhere],
        out_specs=(anywhere, pl.BlockSpec(memory_space=pltpu.VMEM)),
        scratch_shapes=scratch,
        compiler_params=pltpu.CompilerParams(
            collective_id=ident, has_side_effects=True, vmem_limit_bytes=48 << 20
        ),
    )(panel_rank, facs, tokens, cotangent)


def local(sizes, tokens, cotangent, left_factor, right_factor, panel_rank):
    nz, nw, nt = sizes
    facs = jnp.concatenate((left_factor, right_factor), axis=0)
    slots = left_factor.shape[0]
    most = -(-nt * slots // LANES) * LANES
    small = functools.partial(fused, sizes, LANES, 1)
    if most > LANES:
        large = functools.partial(fused, sizes, most, 2)
        grad, home = lax.cond(
            jnp.sum(panel_rank) <= LANES, small, large, panel_rank, facs, tokens, cotangent
        )
    else:
        grad, home = small(panel_rank, facs, tokens, cotangent)
    block = tokens.shape[1] // (nz * nw)
    home = home.transpose(1, 0, 2)[:, :, None, :]
    return (grad, home[..., :block], home[..., block : 2 * block])


def solution(mesh):
    side = math.isqrt(mesh.shape["dp"])
    sizes = (mesh.shape["dp"] // side, side, mesh.shape["tensor"])
    placed = (P("dp", "tensor"), P("dp", "tensor"), P("tensor", None), P("tensor", None), P())
    return jax.shard_map(
        functools.partial(local, sizes),
        mesh=mesh,
        in_specs=placed,
        out_specs=(P("dp", "tensor"), P("tensor", None, "dp", None), P("tensor", None, "dp", None)),
        check_vma=False,
    )
```

time: 167 us -> 79.7 us (0.48)
  blocking collectives: 85.2 us -> 0 us
  Pallas kernels: 0 us -> 72.5 us
  waiting for transfers between devices: 43.1 us -> 0 us
  starting transfers between devices: 16.9 us -> 0 us
  matrix products: 7.49 us -> 0 us
  local copies, waits for them, and re-layouts: 8.95 us -> 2.79 us
  other arithmetic: 4.7 us -> 2.92 us
    pallas_call x0 -> x1, Pallas kernels: none -> 72.5 us  [fused(): pl.pallas_call(functools.partial(kernel, nz, nw, nt, kc, scale), out_shap...]
    all_to_all x1 -> x0, blocking collectives: 54 us -> none  [local(): lax.all_to_all(both, 'dp', split_axis=0, concat_axis=0, tiled=True)]
    all_to_all x2 -> x0, waiting for transfers between devices: 43.1 us -> none  [the longest x1 37.5 us: local(): lax.all_to_all(factors, 'tensor', split_axis=1, concat_axis=0, tiled=True)]
    psum x1 -> x0, blocking collectives: 31.1 us -> none  [local(): hidden, back_hidden = lax.psum((hidden_part, back_part), 'tensor')]
    all_to_all x2 -> x0, starting transfers between devices: 16.9 us -> none  [the longest x1 10.5 us: local(): lax.all_to_all(factors, 'tensor', split_axis=1, concat_axis=0, tiled=True)]
    dot_general x5 -> x0, matrix products: 7.49 us -> none  [the longest x1 2.95 us: local(): lax.dot_general(cotangent, hidden, token_dims, preferred_element_type=jnp...]
    dot_general x2 -> x0, local copies, waits for them, and re-layouts: 3.64 us -> none  [the longest x1 2.21 us: local(): lax.dot_general(cotangent, hidden, token_dims, preferred_element_type=jnp...]
    concatenate x2 -> x1, other arithmetic: 3.45 us -> 1.62 us  [local(): facs = jnp.concatenate((left_factor, right_factor), axis=0)]
  transfers between devices with their start and end apart: 2 -> 0, of which waited for: 2 -> 0; matrix products, arithmetic and copies ran while one was open for 1% -> 0% of each run, Pallas kernels for 0% -> 0%
where the time goes in v2:
time: 79.7 us; the launch traced here: 79.5 us
  Pallas kernels  72.5 us (91%)
  other arithmetic  2.92 us (4%)
  local copies, waits for them, and re-layouts  2.79 us (4%)
  between operations  1.32 us (2%)
    pallas_call x1, Pallas kernels, fused(): pl.pallas_call(functools.partial(kernel, nz, nw, nt, kc, scale), out_shap...  72.5 us
    unnamed x5, local copies, waits for them, and re-layouts  1.86 us
    concatenate x1, other arithmetic, local(): facs = jnp.concatenate((left_factor, right_factor), axis=0)  1.62 us

profile of v2, /device:TPU:1, one launch (start us, length us, event | category | flops | bytes accessed | tf_op | source)
XLA Modules:
  0.0 79.5 jit_solution(6535417535180134382)
XLA Ops:
  0.6 1.3 %reduce_sum.9 = s32[]{:T(128)} reduce(s32[8]{0:T(128)} %param.11, s32[]{:T(128)} %constant.0.clone.1), dimensions={0}, to_apply=%region_0.0 | reduce | flops 7 | bytes 40 | tf_op jit(solution)/shard_map/reduce_sum | solution.py:373
  2.6 0.0 copy-start
  2.6 0.0 copy-start.1
  2.6 1.6 %pad_maximum_fusion = bf16[48,16384]{1,0:T(8,128)(2,1)S(1)} fusion(bf16[24,16384]{1,0:T(8,128)(2,1)} %param.10, bf16[24,16384]{1,0:T(8,128)(2,1)} %param.9), kind=kLoop, calls=%fused_computation | loop fusion | flops 3145728 | bytes 3145728 | tf_op jit(solution)/shard_map/concatenate | solution.py:366
  4.2 0.2 copy-done
  4.5 0.5 copy-done.1
  4.9 72.5 %conditional.1 = ((bf16[384,2048]{1,0:T(8,128)(2,1)S(1)}, f32[8,24,128]{2,1,0:T(8,128)S(1)})) conditional(s32[]{:T(128)} %convert_element_type.3, (s32[8]{0:T(128)}, bf16[48,16384]{1,0:T(8,128)(2,1)S(1)}, bf16[384,2048]{1,0:T(8,128)(2,1)S(1)}, bf16[384,2048]{1,0:T(8,128)(2,1)S(1)}) %tuple.25, (s32[8]{0:T(128)}, bf16[48,16384]{1,0:T(8,128)(2,1)S(1)}, ...), branch_computations={%region_1.0_spmd, %region_2.0_spmd} | conditional | bytes 8 | solution.py:372
  4.9 72.5 %branch_1_fun.1 = (bf16[384,2048]{1,0:T(8,128)(2,1)S(1)}, f32[8,24,128]{2,1,0:T(8,128)S(1)}) custom-call(s32[8]{0:T(128)} %get-tuple-element.20.rank_ref, bf16[48,16384]{1,0:T(8,128)(2,1)S(1)} %get-tuple-element.21.facs, bf16[384,2048]{1,0:T(8,128)(2,1)S(1)} %get-tuple-element.22.tok_hbm, bf16[384,2048]{1,0:T(8,128)(2,1)S(1)} %get-tuple-element.23.cot_hbm), custom_call_target="tpu_custom_call" | custom-call | tf_op jit(solution)/shard_map/cond/branch_1_fun/pallas_call | solution.py:349
  77.5 0.9 %fusion = (f32[24,8,1,32]{3,2,1,0:T(1,128)}, f32[24,8,1,32]{3,2,1,0:T(1,128)}) fusion(f32[24,8,1,128]{3,2,1,0:T(1,128)S(1)} %bitcast.3), kind=kLoop, calls=%fused_computation.1 | loop fusion | bytes 98304 | tf_op jit(solution)/shard_map/slice | solution.py:379
  78.4 1.1 %copy.14 = bf16[384,2048]{1,0:T(8,128)(2,1)} copy(bf16[384,2048]{1,0:T(8,128)(2,1)S(1)} %get-tuple-element.40) | data formatting | bytes 3145728
  (1 shorter events, 0.0 us)
Async XLA Ops:
  2.6 1.9 %copy-start = (bf16[384,2048]{1,0:T(8,128)(2,1)S(1)}, bf16[384,2048]{1,0:T(8,128)(2,1)}, u32[]{:S(2)}) copy-start(bf16[384,2048]{1,0:T(8,128)(2,1)} %param.7) | copy-start | bytes 4718596
  2.6 2.3 %copy-start.1 = (bf16[384,2048]{1,0:T(8,128)(2,1)S(1)}, bf16[384,2048]{1,0:T(8,128)(2,1)}, u32[]{:S(2)}) copy-start(bf16[384,2048]{1,0:T(8,128)(2,1)} %param.8) | copy-start | bytes 4718596

commit v3 on v1

v3 whole, which is shorter than its diff:
```python
import functools
import math

import jax
import jax.numpy as jnp
from jax import lax
from jax.experimental import pallas as pl
from jax.experimental.pallas import tpu as pltpu
from jax.sharding import PartitionSpec as P

LANES = 128
BF16 = jnp.bfloat16
F32 = jnp.float32


def over_rows(a, b):
    return lax.dot_general(a, b, (((0,), (0,)), ((), ())), preferred_element_type=F32)


def over_lanes(a, b):
    return lax.dot_general(a, b, (((1,), (1,)), ((), ())), preferred_element_type=F32)


def kernel(
    nz, nw, nt, kc, scale,
    rank_ref, left_hbm, right_hbm, tok_hbm, cot_hbm,
    tg_hbm, out_ref,
    tok, cot, stage, raw, pick, spread, rows, hid32, hid16, pair_in, pair, quad_in, hidden,
    part_w, part_z, from_w, from_z, sum_w, sum_z, last_z, last_w, piece, home, tgrad,
    loc, ls, a1s, a1r, aws, awr, azs, azr, b1, b2, b3, b4, cws, cwr, czs, czr, dzs, dzr, dws, dwr, es, er,
):
    d = lax.axis_index("dp")
    t = lax.axis_index("tensor")
    z, w = lax.div(d, nw), lax.rem(d, nw)
    yh, core = lax.div(t, 2), lax.rem(t, 2)
    nh, nx = nt // 2, nw // 2
    yl, x = lax.div(w, nx), lax.rem(w, nx)
    k2 = 2 * kc
    tokens, features = tok.shape
    slots = raw.shape[3]
    half = part_w.shape[3]
    nwq = part_w.shape[1]
    nq = nwq + part_z.shape[1]
    split = 3 * kc // 8

    def at_t(k):
        return (d, lax.rem(t + k, nt))

    def at_w(k):
        return (z * nw + lax.rem(w + k, nw), t)

    def at_z(k):
        return (lax.rem(z + k, nz) * nw + w, t)

    def at_h(k):
        return (d, lax.rem(yh + k, nh) * 2 + core)

    mate = (d, t + 1 - 2 * core)

    def describe(src, dst, ssem, rsem, dev):
        return pltpu.make_async_remote_copy(
            src_ref=src, dst_ref=dst, send_sem=ssem, recv_sem=rsem,
            device_id=dev, device_id_type=pl.DeviceIdType.MESH,
        )

    def send(src, dst, ssem, rsem, dev):
        copy = describe(src, dst, ssem, rsem, dev)
        copy.start()
        return copy

    sent = []

    def tiles(column_of):
        return (column_of, nw + column_of, nw + z)

    far = lax.rem(yh + 2, nh)
    ahead, behind = lax.rem(yh + 1, nh), lax.rem(yh + nh - 1, nh)
    near = lax.rem(yh + 2 * yl - 1 + nh, nh)
    targets = [(far, 1 - yl, c, core) for c in range(2)]
    targets += [(near, m, c, 2 + 2 * yl + core) for m in range(2) for c in range(2)]
    targets += [(yh, yl, 1 - core, 6)]
    origins = [2 * far, 2 * far + 1, 2 * ahead, 2 * ahead + 1, 2 * behind, 2 * behind + 1, t + 1 - 2 * core]

    def cut(array, owner, tile):
        return array.at[:, pl.ds(pl.multiple_of(owner * features + tile * LANES, LANES), LANES)]

    sources = (right_hbm, left_hbm)
    local = []
    for side in range(2):
        for i in (2, 0, 1):
            for j, (group, row_of, c, slot) in enumerate(targets):
                tile = tiles(row_of * nx + x)[i]
                local.append(
                    pltpu.make_async_copy(
                        cut(sources[side], group * 2 + c, tile), stage.at[side, i, j], ls.at[side, i, j]
                    )
                )
    for side in range(2):
        for i in range(3):
            local.append(
                pltpu.make_async_copy(cut(sources[side], t, tiles(w)[i]), raw.at[side, i, t], ls.at[side, i, 7])
            )
    load_cot = pltpu.make_async_copy(cot_hbm, cot, loc.at[0])
    load_tok = pltpu.make_async_copy(tok_hbm, tok, loc.at[1])
    for copy in local:
        copy.start()
    load_cot.start()
    load_tok.start()

    barrier = pltpu.get_barrier_semaphore()
    peers = [at_t(k) for k in range(1, nt)]
    peers += [(z * nw + (1 - yl) * nx + x, k) for k in range(nt)]
    peers += [(z * nw + m * nx + lax.rem(x + k, nx), t) for m in range(2) for k in range(1, nx)]
    peers += [at_z(k) for k in range(1, nz)]
    for peer in peers:
        pl.semaphore_signal(barrier, inc=1, device_id=peer, device_id_type=pl.DeviceIdType.MESH)
    pl.semaphore_wait(barrier, len(peers))

    for copy in local:
        copy.wait()
    arrive = [[[], [], []], [[], [], []]]
    for side in range(2):
        for i in (2, 0, 1):
            for j, (group, row_of, c, slot) in enumerate(targets):
                column_of = row_of * nx + x
                dev = (z * nw + column_of, group * 2 + c)
                sent.append(
                    send(stage.at[side, i, j], raw.at[side, i, t], a1s.at[side, j, i], a1r.at[side, slot, i], dev)
                )
                arrive[side][i].append(
                    describe(
                        raw.at[side, i, t], raw.at[side, i, origins[j]], a1s.at[side, j, i], a1r.at[side, j, i], dev
                    )
                )

    slot_c = lax.broadcasted_iota(jnp.int32, (8, nt * slots), 1)
    base_c = jnp.zeros((8, nt * slots), jnp.int32)
    rank_c = jnp.zeros((8, nt * slots), jnp.int32)
    slot_r = lax.broadcasted_iota(jnp.int32, (nt * slots, kc), 0)
    base_r = jnp.zeros((nt * slots, kc), jnp.int32)
    rank_r = jnp.zeros((nt * slots, kc), jnp.int32)
    base = jnp.int32(0)
    for p in range(nt):
        start, stop = base - p * slots, rank_ref[p] + p * slots
        inside = slot_c >= p * slots
        base_c = jnp.where(inside, start, base_c)
        rank_c = jnp.where(inside, stop, rank_c)
        inside = slot_r >= p * slots
        base_r = jnp.where(inside, start, base_r)
        rank_r = jnp.where(inside, stop, rank_r)
        base = base + rank_ref[p]
    row = lax.broadcasted_iota(jnp.int32, (kc, nt * slots), 0)
    place = jnp.where(slot_c < rank_c, base_c + slot_c, -1)[0:1]
    pick[...] = (row == place).astype(F32).astype(BF16)
    col = lax.broadcasted_iota(jnp.int32, (nt * slots, kc), 1)
    spread[...] = ((col == slot_r + base_r) & (slot_r < rank_r)).astype(F32).astype(BF16)

    second = [[], []]

    def picked(side, i, low, high):
        return jnp.dot(
            pick[low:high, :], raw[side, i].reshape(nt * slots, LANES), preferred_element_type=F32
        ).astype(BF16)

    for side in range(2):
        for copy in arrive[side][2]:
            copy.wait_recv()
        rows[side, nw + z, split:kc, :] = picked(side, 2, split, kc)
        for k in range(1, nz):
            ref = rows.at[side, nw + z, split:kc, :]
            second[side].append(send(ref, ref, azs.at[k - 1, side], azr.at[k - 1, side], at_z(k)))
        for copy in arrive[side][0]:
            copy.wait_recv()
        rows[side, w, :, :] = picked(side, 0, 0, kc)
        for k in range(1, nw):
            ref = rows.at[side, w]
            second[side].append(send(ref, ref, aws.at[k - 1, 2 * side], awr.at[k - 1, 2 * side], at_w(k)))
        for copy in arrive[side][1]:
            copy.wait_recv()
        rows[side, nw + w, 0:split, :] = picked(side, 1, 0, split)
        for k in range(1, nw):
            ref = rows.at[side, nw + w, 0:split, :]
            second[side].append(send(ref, ref, aws.at[k - 1, 2 * side + 1], awr.at[k - 1, 2 * side + 1], at_w(k)))
    sent += second[0] + second[1]
    load_cot.wait()
    load_tok.wait()

    share = tokens // nt
    pairs, swaps, shares, relay = [], [[], []], [[], []], []
    arrays = (cot, tok)
    own = core * nh + yh

    def project(side):
        for copy in second[side]:
            copy.wait_recv()
        factor = jnp.concatenate([rows[side, i] for i in range(nw + nz)], axis=1)
        hid32[side] = over_lanes(arrays[side][...], factor).reshape(nt, share, kc)
        hid16[side] = hid32[side, pl.ds((1 - core) * nh, nh)].astype(BF16)
        pairs.append(send(hid16.at[side], pair_in.at[side], b1.at[0, side], b1.at[1, side], mate))

    def pair_up(side):
        pairs[side].wait_recv()
        pair[side] = (hid32[side, pl.ds(core * nh, nh)] + pair_in[side].astype(F32)).astype(BF16)
        for k in range(1, nh):
            to = lax.rem(yh + k, nh)
            swaps[side].append(
                send(pair.at[side, to], quad_in.at[side, k - 1], b2.at[0, side, k - 1], b2.at[1, side, k - 1], at_h(k))
            )

    def settle(side):
        total = hid32[side, own] + pair_in[side, yh].astype(F32)
        for k in range(1, nh):
            swaps[side][k - 1].wait_recv()
            total = total + quad_in[side, k - 1].astype(F32)
        hidden[side, own] = total.astype(BF16)
        for k in range(1, nh):
            ref = hidden.at[side, own]
            shares[side].append(send(ref, ref, b3.at[0, side, k - 1], b3.at[1, side, k - 1], at_h(k)))

    def pass_on(side):
        for copy in shares[side]:
            copy.wait_recv()
        ref = hidden.at[side, pl.ds(core * nh, nh)]
        relay.append(send(ref, ref, b4.at[0, side], b4.at[1, side], mate))

    project(0)
    pair_up(0)
    project(1)
    pair_up(1)
    settle(0)
    settle(1)
    pass_on(0)

    zone = features // nz
    tiles_k = kc // LANES

    def outer(array, columns, slab):
        for zb in range(nz):
            full = over_rows(array[:, zb * zone : (zb + 1) * zone], columns).astype(BF16)
            full = full.reshape(nw, 2, half, kc)
            for j in range(tiles_k):
                for h in range(2):
                    q = slab + 2 * j + h
                    value = full[:, h, :, j * LANES : (j + 1) * LANES]
                    if q < nwq:
                        part_w[:, q, zb] = value
                    else:
                        part_z[zb, q - nwq] = value

    relay[0].wait_recv()
    back = hidden[0].reshape(tokens, kc)
    outer(tok, back, 0)
    third_w, third_z = [], []
    for k in range(1, nw):
        to = lax.rem(w + k, nw)
        third_w.append(
            send(part_w.at[to, 0 : nq // 2], from_w.at[k - 1, 0 : nq // 2], cws.at[k - 1, 0], cwr.at[k - 1, 0], at_w(k))
        )
    pass_on(1)
    for i in range(0, nw + nz, 2):
        both = jnp.concatenate([rows[1, i], rows[1, i + 1]], axis=1)
        tgrad[:, i * LANES : (i + 2) * LANES] = jnp.dot(back, both, preferred_element_type=F32).astype(BF16)
    store_tg = pltpu.make_async_copy(tgrad, tg_hbm, loc.at[2])
    store_tg.start()
    relay[1].wait_recv()
    sent += pairs + swaps[0] + swaps[1] + shares[0] + shares[1] + relay
    outer(cot, hidden[1].reshape(tokens, kc), nq // 2)
    for k in range(1, nz):
        to = lax.rem(z + k, nz)
        third_z.append(send(part_z.at[to], from_z.at[k - 1], czs.at[k - 1], czr.at[k - 1], at_z(k)))
    for k in range(1, nw):
        to = lax.rem(w + k, nw)
        third_w.append(
            send(part_w.at[to, nq // 2 : nwq], from_w.at[k - 1, nq // 2 : nwq], cws.at[k - 1, 1], cwr.at[k - 1, 1], at_w(k))
        )
    sent += third_w + third_z

    fourth = [[], []]
    for side, low, high in ((0, 0, nq // 2), (1, nq // 2, nwq)):
        for copy in third_w[side * (nw - 1) : (side + 1) * (nw - 1)]:
            copy.wait_recv()
        for q in range(low, high):
            total = part_w[w, q].astype(F32)
            for k in range(1, nw):
                total = total + from_w[k - 1, q].astype(F32)
            sum_w[:, q] = total.astype(BF16)
        for k in range(1, nz):
            to = lax.rem(z + k, nz)
            fourth[side].append(
                send(sum_w.at[to, low:high], last_z.at[k - 1, low:high], dzs.at[k - 1, side], dzr.at[k - 1, side], at_z(k))
            )
    for copy in third_z:
        copy.wait_recv()
    total = part_z[z].astype(F32)
    for k in range(1, nz):
        total = total + from_z[k - 1].astype(F32)
    for q in range(nq - nwq):
        sum_z[:, q] = total[q].astype(BF16)
    for k in range(1, nw):
        to = lax.rem(w + k, nw)
        fourth[1].append(send(sum_z.at[to], last_w.at[k - 1], dws.at[k - 1], dwr.at[k - 1], at_w(k)))
    sent += fourth[0] + fourth[1]

    def slab(q):
        if q < nwq:
            total = sum_w[z, q].astype(F32)
            for k in range(1, nz):
                total = total + last_z[k - 1, q].astype(F32)
        else:
            total = sum_z[w, q - nwq].astype(F32)
            for k in range(1, nw):
                total = total + last_w[k - 1, q - nwq].astype(F32)
        return total * scale

    chosen = spread[...]
    fifth = []
    for side in range(2):
        for copy in fourth[side]:
            copy.wait_recv()
        first = side * nq // 2
        final = jnp.concatenate(
            [jnp.concatenate([slab(first + 2 * j), slab(first + 2 * j + 1)], axis=0) for j in range(tiles_k)], axis=1
        )
        spare = piece.shape[3] - 2 * half
        if spare:
            final = jnp.concatenate([final, jnp.zeros((spare, kc), F32)], axis=0)
        high = final.astype(BF16)
        rest = final - high.astype(F32)
        middle = rest.astype(BF16)
        low = (rest - middle.astype(F32)).astype(BF16)
        placed = over_lanes(chosen, high) + over_lanes(chosen, middle) + over_lanes(chosen, low)
        piece[side] = placed.reshape(nt, slots, piece.shape[3])
        for k in range(1, nt):
            to = lax.rem(t + k, nt)
            fifth.append(send(piece.at[side, to], home.at[side, t], es.at[k - 1, side], er.at[k - 1, side], at_t(k)))
        home[side, t] = piece[side, t]
    for copy in fifth:
        copy.wait_recv()
    out_ref[...] = home[...]
    sent += fifth
    for copy in sent:
        copy.wait_send()
    store_tg.wait()


def fused(sizes, kc, ident, panel_rank, left_factor, right_factor, tokens, cotangent):
    nz, nw, nt = sizes
    count, features = tokens.shape
    slots = left_factor.shape[0]
    k2 = 2 * kc
    nq = 2 * k2 // LANES
    nwq = 3 * nq // 4
    half = features // (nz * nw * 2)
    wide = max(LANES, 2 * half)
    share = count // nt
    nh = nt // 2
    scale = 1.0 / math.sqrt(count * nz * nw)
    dma = pltpu.SemaphoreType.DMA
    vmem = pltpu.VMEM
    scratch = [
        vmem((count, features), BF16),
        vmem((count, features), BF16),
        vmem((2, 3, 7, slots, LANES), BF16),
        vmem((2, 3, nt, slots, LANES), BF16),
        vmem((kc, nt * slots), BF16),
        vmem((nt * slots, kc), BF16),
        vmem((2, nw + nz, kc, LANES), BF16),
        vmem((2, nt, share, kc), F32),
        vmem((2, nh, share, kc), BF16),
        vmem((2, nh, share, kc), BF16),
        vmem((2, nh, share, kc), BF16),
        vmem((2, nh - 1, share, kc), BF16),
        vmem((2, nt, share, kc), BF16),
        vmem((nw, nwq, nz, half, LANES), BF16),
        vmem((nz, nq - nwq, nw, half, LANES), BF16),
        vmem((nw - 1, nwq, nz, half, LANES), BF16),
        vmem((nz - 1, nq - nwq, nw, half, LANES), BF16),
        vmem((nz, nwq, half, LANES), BF16),
        vmem((nw, nq - nwq, half, LANES), BF16),
        vmem((nz - 1, nwq, half, LANES), BF16),
        vmem((nw - 1, nq - nwq, half, LANES), BF16),
        vmem((2, nt, slots, wide), F32),
        vmem((2, nt, slots, wide), F32),
        vmem((count, features), BF16),
        dma((3,)),
        dma((2, 3, 8)),
        dma((2, 7, 3)),
        dma((2, 7, 3)),
        dma((nw - 1, 4)),
        dma((nw - 1, 4)),
        dma((nz - 1, 2)),
        dma((nz - 1, 2)),
        dma((2, 2)),
        dma((2, 2, nh - 1)),
        dma((2, 2, nh - 1)),
        dma((2, 2)),
        dma((nw - 1, 2)),
        dma((nw - 1, 2)),
        dma((nz - 1,)),
        dma((nz - 1,)),
        dma((nz - 1, 2)),
        dma((nz - 1, 2)),
        dma((nw - 1,)),
        dma((nw - 1,)),
        dma((nt - 1, 2)),
        dma((nt - 1, 2)),
    ]
    anywhere = pl.BlockSpec(memory_space=pl.ANY)
    return pl.pallas_call(
        functools.partial(kernel, nz, nw, nt, kc, scale),
        out_shape=(
            jax.ShapeDtypeStruct((count, features), BF16),
            jax.ShapeDtypeStruct((2, nt, slots, wide), F32),
        ),
        in_specs=[pl.BlockSpec(memory_space=pltpu.SMEM), anywhere, anywhere, anywhere, anywhere],
        out_specs=(anywhere, pl.BlockSpec(memory_space=pltpu.VMEM)),
        scratch_shapes=scratch,
        compiler_params=pltpu.CompilerParams(
            collective_id=ident, has_side_effects=True, vmem_limit_bytes=48 << 20
        ),
    )(panel_rank, left_factor, right_factor, tokens, cotangent)


def local(sizes, tokens, cotangent, left_factor, right_factor, panel_rank):
    nz, nw, nt = sizes
    slots = left_factor.shape[0]
    most = -(-nt * slots // LANES) * LANES
    small = functools.partial(fused, sizes, LANES, 1)
    if most > LANES:
        large = functools.partial(fused, sizes, most, 2)
        grad, home = lax.cond(
            jnp.sum(panel_rank) <= LANES, small, large, panel_rank, left_factor, right_factor, tokens, cotangent
        )
    else:
        grad, home = small(panel_rank, left_factor, right_factor, tokens, cotangent)
    block = tokens.shape[1] // (nz * nw)
    home = home[..., :block].transpose(0, 2, 1, 3)[:, :, :, None, :]
    return (grad, home[0], home[1])


def solution(mesh):
    side = math.isqrt(mesh.shape["dp"])
    sizes = (mesh.shape["dp"] // side, side, mesh.shape["tensor"])
    placed = (P("dp", "tensor"), P("dp", "tensor"), P("tensor", None), P("tensor", None), P())
    return jax.shard_map(
        functools.partial(local, sizes),
        mesh=mesh,
        in_specs=placed,
        out_specs=(P("dp", "tensor"), P("tensor", None, "dp", None), P("tensor", None, "dp", None)),
        check_vma=False,
    )
```

time: 167 us -> 71.4 us (0.43)
  blocking collectives: 85.2 us -> 0 us
  Pallas kernels: 0 us -> 66.8 us
  waiting for transfers between devices: 43.1 us -> 0 us
  starting transfers between devices: 16.9 us -> 0 us
  matrix products: 7.49 us -> 0 us
  local copies, waits for them, and re-layouts: 8.95 us -> 1.88 us
  other arithmetic: 4.7 us -> 1.29 us
    pallas_call x0 -> x1, Pallas kernels: none -> 66.8 us  [fused(): pl.pallas_call(functools.partial(kernel, nz, nw, nt, kc, scale), out_shap...]
    all_to_all x1 -> x0, blocking collectives: 54 us -> none  [local(): lax.all_to_all(both, 'dp', split_axis=0, concat_axis=0, tiled=True)]
    all_to_all x2 -> x0, waiting for transfers between devices: 43.1 us -> none  [the longest x1 37.5 us: local(): lax.all_to_all(factors, 'tensor', split_axis=1, concat_axis=0, tiled=True)]
    psum x1 -> x0, blocking collectives: 31.1 us -> none  [local(): hidden, back_hidden = lax.psum((hidden_part, back_part), 'tensor')]
    all_to_all x2 -> x0, starting transfers between devices: 16.9 us -> none  [the longest x1 10.5 us: local(): lax.all_to_all(factors, 'tensor', split_axis=1, concat_axis=0, tiled=True)]
    dot_general x5 -> x0, matrix products: 7.49 us -> none  [the longest x1 2.95 us: local(): lax.dot_general(cotangent, hidden, token_dims, preferred_element_type=jnp...]
    dot_general x2 -> x0, local copies, waits for them, and re-layouts: 3.64 us -> none  [the longest x1 2.21 us: local(): lax.dot_general(cotangent, hidden, token_dims, preferred_element_type=jnp...]
    concatenate x2 -> x0, other arithmetic: 3.45 us -> none  [the longest x1 1.86 us: local(): both = jnp.concatenate((left_t, right_t), axis=1).astype(jnp.bfloat16)]
  transfers between devices with their start and end apart: 2 -> 0, of which waited for: 2 -> 0; matrix products, arithmetic and copies ran while one was open for 1% -> 0% of each run, Pallas kernels for 0% -> 0%
where the time goes in v3:
time: 71.4 us; the launch traced here: 71.3 us
  Pallas kernels  66.8 us (94%)
  local copies, waits for them, and re-layouts  1.88 us (3%)
  between operations  1.31 us (2%)
  other arithmetic  1.29 us (2%)
    pallas_call x1, Pallas kernels, fused(): pl.pallas_call(functools.partial(kernel, nz, nw, nt, kc, scale), out_shap...  66.8 us

profile of v3, /device:TPU:1, one launch (start us, length us, event | category | flops | bytes accessed | tf_op | source)
XLA Modules:
  0.0 71.3 jit_solution(3211182883597539046)
XLA Ops:
  0.6 1.3 %reduce_sum.9 = s32[]{:T(128)} reduce(s32[8]{0:T(128)} %param.11, s32[]{:T(128)} %constant.0.clone.1), dimensions={0}, to_apply=%region_0.0 | reduce | flops 7 | bytes 40 | tf_op jit(solution)/shard_map/reduce_sum | solution.py:432
  2.6 66.8 %conditional.1 = ((bf16[384,2048]{1,0:T(8,128)(2,1)S(1)}, f32[2,8,24,128]{3,2,1,0:T(8,128)S(1)})) conditional(s32[]{:T(128)} %convert_element_type.3, (s32[8]{0:T(128)}, bf16[24,16384]{1,0:T(8,128)(2,1)}, bf16[24,16384]{1,0:T(8,128)(2,1)}, bf16[384,2048]{1,0:T(8,128)(2,1)}, bf16[384,2048]{1,0:T(8,128)(2,1)}) %tuple.14, (s32[8]{0:T(128)}, ...), branch_computations={%region_1.0_spmd, %region_2.0_spmd} | conditional | bytes 8 | solution.py:431
  2.6 66.8 %branch_1_fun.1 = (bf16[384,2048]{1,0:T(8,128)(2,1)S(1)}, f32[2,8,24,128]{3,2,1,0:T(8,128)S(1)}) custom-call(s32[8]{0:T(128)} %get-tuple-element.25.rank_ref, bf16[24,16384]{1,0:T(8,128)(2,1)} %get-tuple-element.26.left_hbm, bf16[24,16384]{1,0:T(8,128)(2,1)} %get-tuple-element.27.right_hbm, bf16[384,2048]{1,0:T(8,128)(2,1)} %get-tuple-element.28.tok_hbm, ...), custom_call_target="tpu_custom_call" | custom-call | tf_op jit(solution)/shard_map/cond/branch_1_fun/pallas_call | solution.py:409
  69.5 0.7 fusion
  70.1 1.1 %copy.14 = bf16[384,2048]{1,0:T(8,128)(2,1)} copy(bf16[384,2048]{1,0:T(8,128)(2,1)S(1)} %get-tuple-element.46) | data formatting | bytes 3145728
  (2 shorter events, 0.1 us)
